TPU v7x, 256 devices: a whole 4x4x8 slice. The times are simulated.
256 devices in a mesh: az: 128 (over z, y, x_hi, core), rd: 2 (over x_lo).
Axes of the slice: x: 4 (x_hi: 2, x_lo: 2; x = x_hi * 2 + x_lo), y: 4, z: 8, core: 2. Of those that a mesh axis runs over, the one named last changes fastest.
Arguments:
- echoes: bfloat16 [2, 2048, 32, 2048], P(None, 'az', None, 'rd'), may hold values from -6 to 6
- pulse_taper: float32 [32], replicated, may hold values from 0.1 to 1.9
- beam_weights: float32 [5], replicated, may hold values from 0.3 to 1
- blanking: int32 [2048, 16], P('az'), may hold values 0 or 1
- cfar_sizes: int32 [6], replicated, may hold values from 1 to 23, as said below
Outputs:
- detection: bfloat16 [2048, 32, 2048], P('az', 'rd')
Inputs may be any that keep to these rules, and one draw needn't show every extreme that they name: `cfar_sizes`: the range guard (entry 0) is 1; the Doppler and azimuth guards (entries 2, 4) are 1 or 2; guard plus window is exactly 24 for range (entries 0, 1), 4 for Doppler (2, 3) and 12 for azimuth (4, 5).
All inputs are finite; a program needn't handle non-finite values. No bound on the sum of `blanking` on one device may be relied on, other than what follows from the above.
Results may differ from a plain program's by a relative error of at most 0.012.
Values may be sent and summed in bfloat16 or wider, within the bound.
A program may use at most 64 MiB of HBM per device.

v0:
```python
import math

import jax
import jax.numpy as jnp
from jax import lax
from jax.sharding import PartitionSpec as P

REACH_R = 24
REACH_D = 4
REACH_A = 12
BLANK_CELLS = 128


def with_halo(cells, sides, width, closed):
    for axis, dim in sides:
        count = lax.axis_size(axis)
        ends = count if closed else count - 1
        head = lax.slice_in_dim(cells, 0, width, axis=dim)
        tail = lax.slice_in_dim(cells, cells.shape[dim] - width, cells.shape[dim], axis=dim)
        cells = jnp.concatenate(
            [
                lax.ppermute(tail, axis, [(i, (i + 1) % count) for i in range(ends)]),
                cells,
                lax.ppermute(head, axis, [((i + 1) % count, i) for i in range(ends)]),
            ],
            axis=dim,
        )
    return cells


def bank_matrix(pulse_taper):
    pulses = pulse_taper.shape[0]
    indices = jnp.arange(pulses, dtype=jnp.int32)
    phases = indices[:, None] * indices[None, :] % pulses
    angles = phases.astype(jnp.float32) * (2.0 * math.pi / pulses)
    cosines = jnp.cos(angles) * pulse_taper[None, :]
    sine_terms = jnp.sin(angles) * pulse_taper[None, :]
    real_row = jnp.stack([cosines, sine_terms], axis=1)
    imag_row = jnp.stack([-sine_terms, cosines], axis=1)
    return jnp.stack([real_row, imag_row], axis=0).astype(jnp.bfloat16)


def window_bands(extended, length, reach, guard):
    rows_index = lax.broadcasted_iota(jnp.int32, (extended, length), 0)
    cols_index = lax.broadcasted_iota(jnp.int32, (extended, length), 1)
    before = cols_index + reach - rows_index
    after = rows_index - cols_index - reach
    leading = ((before > guard) & (before <= reach)).astype(jnp.bfloat16)
    lagging = ((after > guard) & (after <= reach)).astype(jnp.bfloat16)
    return (leading, lagging)


def local(echoes, pulse_taper, beam_weights, blanking, cfar_sizes):
    pulses = pulse_taper.shape[0]
    dwells = echoes.shape[1]
    bank = bank_matrix(pulse_taper)
    spectrum = jnp.einsum("ckdp,dapr->cakr", bank, echoes, preferred_element_type=jnp.float32)
    powers = (spectrum[0] * spectrum[0] + spectrum[1] * spectrum[1]) / pulses
    margin = 0
    beside_all = with_halo(powers, (("az", 0),), 2, True)
    span = dwells + 2 * margin
    integrated = beam_weights[0] * beside_all[0:span]
    for offset in range(1, 5):
        integrated = integrated + beam_weights[offset] * beside_all[offset : offset + span]
    log_power = jnp.log(integrated + 0.05).astype(jnp.bfloat16)
    log_power = with_halo(log_power, (("az", 0),), REACH_A, True)
    center = log_power[REACH_A : REACH_A + dwells]
    local_bins = center.shape[1]
    local_cells = center.shape[2]
    guard_range = cfar_sizes[0]
    guard_doppler = cfar_sizes[2]
    window_doppler = cfar_sizes[3].astype(jnp.float32)
    guard_azimuth = cfar_sizes[4]
    window_azimuth = cfar_sizes[5].astype(jnp.float32)
    lead_band, lag_band = window_bands(dwells + 2 * REACH_A, dwells, REACH_A, guard_azimuth)
    azimuth_lead = (
        jnp.einsum("sb,sqr->bqr", lead_band, log_power, preferred_element_type=jnp.float32)
        / window_azimuth
    )
    azimuth_lag = (
        jnp.einsum("sb,sqr->bqr", lag_band, log_power, preferred_element_type=jnp.float32)
        / window_azimuth
    )
    offset_cells = lax.axis_index("rd") * local_cells
    total_cells = local_cells * lax.axis_size("rd")
    widened = with_halo(center, (("rd", 2),), REACH_R, False)
    positions = offset_cells - REACH_R + jnp.arange(local_cells + 2 * REACH_R, dtype=jnp.int32)
    inside = ((positions >= 0) & (positions < total_cells)).astype(jnp.float32)
    block_count = blanking.shape[1]
    block_ids = jnp.clip(positions // BLANK_CELLS, 0, block_count - 1)
    selector = (block_ids[None, :] == jnp.arange(block_count, dtype=jnp.int32)[:, None]).astype(
        jnp.float32
    )
    weight = (
        jnp.dot(blanking.astype(jnp.float32), selector, precision=lax.Precision.HIGHEST)
        * inside[None, :]
    )
    weighted = widened * weight[:, None, :].astype(jnp.bfloat16)
    pieces = local_cells // BLANK_CELLS
    extent = BLANK_CELLS + 2 * REACH_R
    value_blocks = jnp.stack(
        [
            weighted[:, :, number * BLANK_CELLS : number * BLANK_CELLS + extent]
            for number in range(pieces)
        ],
        axis=2,
    )
    weight_blocks = jnp.stack(
        [
            weight[:, number * BLANK_CELLS : number * BLANK_CELLS + extent]
            for number in range(pieces)
        ],
        axis=1,
    )
    range_lead_band, range_lag_band = window_bands(extent, BLANK_CELLS, REACH_R, guard_range)

    def range_mean(banded):
        sums = jnp.einsum("aqbs,sr->aqbr", value_blocks, banded, preferred_element_type=jnp.float32)
        sums = sums.reshape(dwells, local_bins, local_cells)
        counts = jnp.einsum(
            "abs,sr->abr",
            weight_blocks,
            banded.astype(jnp.float32),
            precision=lax.Precision.HIGHEST,
        )
        counts = counts.reshape(dwells, local_cells)
        return sums / jnp.maximum(counts, 1.0)[:, None, :]

    range_lead = range_mean(range_lead_band)
    range_lag = range_mean(range_lag_band)
    circled = jnp.concatenate(
        [center[:, local_bins - REACH_D :], center, center[:, :REACH_D]], axis=1
    )
    doppler_lead_band, doppler_lag_band = window_bands(
        local_bins + 2 * REACH_D, local_bins, REACH_D, guard_doppler
    )
    doppler_lead = (
        jnp.einsum("asr,sk->akr", circled, doppler_lead_band, preferred_element_type=jnp.float32)
        / window_doppler
    )
    doppler_lag = (
        jnp.einsum("asr,sk->akr", circled, doppler_lag_band, preferred_element_type=jnp.float32)
        / window_doppler
    )
    noise_level = jnp.maximum(
        jnp.maximum(range_lead, range_lag), jnp.maximum(doppler_lead, doppler_lag)
    )
    noise_level = jnp.maximum(noise_level, jnp.maximum(azimuth_lead, azimuth_lag))
    keep = weight[:, REACH_R : REACH_R + local_cells]
    detection = (keep[:, None, :] * (center.astype(jnp.float32) - noise_level)).astype(jnp.bfloat16)
    detection = lax.all_to_all(detection, "rd", split_axis=1, concat_axis=2, tiled=True)
    return detection


def solution(mesh):
    in_specs = (P(None, "az", None, "rd"), P(), P(), P("az", None), P())
    out_specs = P("az", "rd", None)
    return jax.shard_map(local, mesh=mesh, in_specs=in_specs, out_specs=out_specs, check_vma=False)
```

profile of v0, /device:TPU:1, one launch (start us, length us, event | category | flops | bytes accessed | tf_op | source)
XLA Modules:
  0.0 95.5 jit_solution(6288917200939661095)
XLA Ops:
  0.0 0.7 fusion.75
  0.8 2.3 %convolution_bitcast_fusion = f32[2,16,32,1024]{3,2,1,0:T(8,128)S(1)} fusion(bf16[2,16,32,1024]{3,2,1,0:T(8,128)(2,1)} %param.5, bf16[1,32,2,32]{3,1,2,0:T(8,128)(2,1)S(1)} %get-tuple-element.14, bf16[1,32,2,32]{3,1,2,0:T(8,128)(2,1)S(1)} %get-tuple-element.13), kind=kOutput, calls=%fused_computation.11 | convolution fusion | flops 134234112 | bytes 6299648 | tf_op jit(solution)/shard_map/ckdp,dapr->cakr/dot_general | solution.py:57
  3.1 0.0 copy-start
  3.1 0.7 broadcast_multiply_fusion
  3.8 3.3 %collective-permute-start.1 = (f32[2,32,1024]{2,1,0:T(8,128)S(1)}, f32[2,32,1024]{2,1,0:T(8,128)S(1)}, u32[]{:S(2)}, u32[]{:S(2)}) collective-permute-start(f32[2,32,1024]{2,1,0:T(8,128)S(1)} %get-tuple-element.6), channel_id=1, source_target_pairs={{2,0},{4,2},{6,4},{8,6},{10,8},{12,10},{14,12},{16,14},{18,16},{20... | collective-permute-start | bytes 786440 | tf_op jit(solution)/shard_map/ppermute | solution.py:24
  7.1 1.0 %collective-permute-start = (f32[2,32,1024]{2,1,0:T(8,128)S(1)}, f32[2,32,1024]{2,1,0:T(8,128)S(1)}, u32[]{:S(2)}, u32[]{:S(2)}) collective-permute-start(f32[2,32,1024]{2,1,0:T(8,128)S(1)} %get-tuple-element.5), channel_id=1, source_target_pairs={{0,2},{2,4},{4,6},{6,8},{8,10},{10,12},{12,14},{14,16},{16,18},{18... | collective-permute-start | bytes 786440 | tf_op jit(solution)/shard_map/ppermute | solution.py:22
  8.1 0.0 copy-done
  8.2 0.5 fusion.129
  8.7 0.0 copy-done.6
  8.7 0.7 fusion.127
  9.3 0.6 fusion.126
  10.0 0.0 copy-done.8
  10.0 0.2 fusion.128
  10.2 0.9 convolution_maximum_fusion
  11.1 0.9 convolution_maximum_fusion.1
  12.0 0.1 slice.178
  14.0 0.7 copy_bitcast_fusion
  14.6 0.0 collective-permute-done.1
  14.7 2.0 %collective-permute-done = f32[2,32,1024]{2,1,0:T(8,128)S(1)} collective-permute-done((f32[2,32,1024]{2,1,0:T(8,128)S(1)}, f32[2,32,1024]{2,1,0:T(8,128)S(1)}, u32[]{:S(2)}, u32[]{:S(2)}) %collective-permute-start) | collective-permute-done | bytes 262176 | tf_op jit(solution)/shard_map/ppermute | solution.py:22
  16.6 0.7 copy-done.3
  17.3 5.8 %fusion.11 = bf16[16,32,1024]{2,1,0:T(8,128)(2,1)S(1)} fusion(f32[16,32,1024]{2,1,0:T(8,128)S(1)} %fusion.129, f32[2,32,1024]{2,1,0:T(8,128)S(1)} %collective-permute-done.1, f32[2,32,1024]{2,1,0:T(8,128)} %copy-done.3, f32[]{:T(128)} %bitcast.18, f32[]{:T(128)} %bitcast.16, f32[]{:T(128)} %bitcast.14, f32[]{:T(128)} %bitcast.13, f32[]{:T(128)} %bitcast.1, ...), kind=kLoop, calls=%fused_computation.18 | loop fusion | flops 9437184 | bytes 7864340 | tf_op jit(solution)/shard_map/convert_element_type | solution.py:65
  23.2 1.3 %fusion.125 = (bf16[12,32,1024]{2,1,0:T(8,128)(2,1)}, bf16[12,32,1024]{2,1,0:T(8,128)(2,1)}) fusion(bf16[16,32,1024]{2,1,0:T(8,128)(2,1)S(1)} %fusion.11), kind=kLoop, calls=%fused_computation.187 | loop fusion | bytes 3145728 | tf_op jit(solution)/shard_map/slice | solution.py:19
  24.5 0.1 fusion.124
  24.6 0.1 fusion.123
  24.7 10.6 %collective-permute-start.5 = (bf16[12,32,1024]{2,1,0:T(8,128)(2,1)}, bf16[12,32,1024]{2,1,0:T(8,128)(2,1)}, u32[]{:S(2)}, u32[]{:S(2)}) collective-permute-start(bf16[12,32,1024]{2,1,0:T(8,128)(2,1)} %get-tuple-element.12), channel_id=1, source_target_pairs={{2,0},{4,2},{6,4},{8,6},{10,8},{12,10},{14,12},{16,14},{18,16},{20... | collective-permute-start | bytes 2359304 | tf_op jit(solution)/shard_map/ppermute | solution.py:24
  35.3 0.0 collective-permute-start.4
  35.3 2.2 %collective-permute-start.2 = (bf16[16,32,24]{2,1,0:T(8,128)(2,1)S(1)}, bf16[16,32,24]{2,1,0:T(8,128)(2,1)S(1)}, u32[]{:S(2)}, u32[]{:S(2)}) collective-permute-start(bf16[16,32,24]{2,1,0:T(8,128)(2,1)S(1)} %get-tuple-element.8), channel_id=1, source_target_pairs={{0,1},{2,3},{4,5},{6,7},{8,9},{10,11},{12,13},{14,15},{16,17},{18,... | collective-permute-start | bytes 73736 | tf_op jit(solution)/shard_map/ppermute | solution.py:22
  37.5 1.5 %collective-permute-start.3 = (bf16[16,32,24]{2,1,0:T(8,128)(2,1)S(1)}, bf16[16,32,24]{2,1,0:T(8,128)(2,1)S(1)}, u32[]{:S(2)}, u32[]{:S(2)}) collective-permute-start(bf16[16,32,24]{2,1,0:T(8,128)(2,1)S(1)} %get-tuple-element.7), channel_id=1, source_target_pairs={{1,0},{3,2},{5,4},{7,6},{9,8},{11,10},{13,12},{15,14},{17,16},{19,... | collective-permute-start | bytes 73736 | tf_op jit(solution)/shard_map/ppermute | solution.py:24
  39.0 2.6 %fusion.30 = f32[32,16,1024]{2,0,1:T(8,128)} fusion(bf16[16,4,1024]{2,1,0:T(4,128)(2,1)S(1)} %get-tuple-element.10, bf16[16,32,1024]{2,1,0:T(8,128)(2,1)S(1)} %fusion.11, bf16[16,4,1024]{2,1,0:T(4,128)(2,1)S(1)} %get-tuple-element.9, s32[]{:T(128)} %bitcast.42, s32[32]{0:T(128)S(1)} %iota_add_fusion.2), kind=kOutput, calls=%fused_computation.47 | convolution fusion | flops 45880320 | bytes 3408004 | tf_op jit(solution)/shard_map/asr,sk->akr/dot_general | solution.py:138
  41.6 11.1 %collective-permute-done.2 = bf16[16,32,24]{2,1,0:T(8,128)(2,1)S(1)} collective-permute-done((bf16[16,32,24]{2,1,0:T(8,128)(2,1)S(1)}, bf16[16,32,24]{2,1,0:T(8,128)(2,1)S(1)}, u32[]{:S(2)}, u32[]{:S(2)}) %collective-permute-start.2) | collective-permute-done | bytes 24608 | tf_op jit(solution)/shard_map/ppermute | solution.py:22
  52.7 1.1 %collective-permute-done.3 = bf16[16,32,24]{2,1,0:T(8,128)(2,1)S(1)} collective-permute-done((bf16[16,32,24]{2,1,0:T(8,128)(2,1)S(1)}, bf16[16,32,24]{2,1,0:T(8,128)(2,1)S(1)}, u32[]{:S(2)}, u32[]{:S(2)}) %collective-permute-start.3) | collective-permute-done | bytes 24608 | tf_op jit(solution)/shard_map/ppermute | solution.py:24
  53.9 1.9 %concatenate.20 = bf16[16,32,1072]{2,1,0:T(8,128)(2,1)S(1)} concatenate(bf16[16,32,24]{2,1,0:T(8,128)(2,1)S(1)} %collective-permute-done.2, bf16[16,32,1024]{2,1,0:T(8,128)(2,1)S(1)} %fusion.11, bf16[16,32,24]{2,1,0:T(8,128)(2,1)S(1)} %collective-permute-done.3), dimensions={2} | concatenate | bytes 2195456 | tf_op jit(solution)/shard_map/concatenate | solution.py:20
  55.8 0.1 broadcast_multiply_fusion.1
  56.1 3.3 %fusion.26 = f32[16,32,8,128]{3,2,1,0:T(8,128)} fusion(bf16[16,32,8,176]{3,1,0,2:T(8,128)(2,1)S(1)} %fusion.31, s32[]{:T(128)} %bitcast.27), kind=kOutput, calls=%fused_computation.40 | convolution fusion | flops 184662016 | bytes 3538948 | tf_op jit(solution)/shard_map/aqbs,sr->aqbr/dot_general | solution.py:118
  59.4 2.7 %reshape.196 = f32[16,32,1024]{2,1,0:T(8,128)} reshape(f32[16,32,8,128]{3,2,1,0:T(8,128)} %fusion.26) | data formatting | bytes 4194304 | tf_op jit(solution)/shard_map/reshape | solution.py:119
  62.1 3.3 %fusion.28 = f32[16,32,8,128]{3,2,1,0:T(8,128)} fusion(bf16[16,32,8,176]{3,1,0,2:T(8,128)(2,1)S(1)} %fusion.31, s32[]{:T(128)} %bitcast.27, s32[128]{0:T(128)S(1)} %iota_add_fusion.3), kind=kOutput, calls=%fused_computation.42 | convolution fusion | flops 184639488 | bytes 3539460 | tf_op jit(solution)/shard_map/aqbs,sr->aqbr/dot_general | solution.py:118
  65.4 1.7 %reshape.195 = f32[16,32,1024]{2,1,0:T(8,128)S(1)} reshape(f32[16,32,8,128]{3,2,1,0:T(8,128)} %fusion.28) | data formatting | bytes 4194304 | tf_op jit(solution)/shard_map/reshape | solution.py:119
  67.2 0.0 collective-permute-done.5
  67.2 0.0 collective-permute-done.4
  67.2 1.7 %pad_maximum_fusion = bf16[40,32,1024]{2,1,0:T(8,128)(2,1)S(1)} fusion(bf16[12,32,1024]{2,1,0:T(8,128)(2,1)} %collective-permute-done.5, bf16[16,32,1024]{2,1,0:T(8,128)(2,1)S(1)} %fusion.11, bf16[12,32,1024]{2,1,0:T(8,128)(2,1)} %collective-permute-done.4), kind=kLoop, calls=%fused_computation | loop fusion | flops 2621440 | bytes 5242880 | tf_op jit(solution)/shard_map/concatenate | solution.py:20
  68.8 3.7 %fusion = f32[16,32,1024]{2,0,1:T(8,128)S(1)} fusion(bf16[40,32,1024]{2,1,0:T(8,128)(2,1)S(1)} %pad_maximum_fusion, s32[]{:T(128)} %bitcast.47), kind=kOutput, calls=%fused_computation.5 | convolution fusion | flops 41946240 | bytes 4718596 | tf_op jit(solution)/shard_map/sb,sqr->bqr/dot_general | solution.py:81
  72.6 3.9 %fusion.2 = f32[16,32,1024]{2,0,1:T(8,128)S(1)} fusion(bf16[40,32,1024]{2,1,0:T(8,128)(2,1)S(1)} %pad_maximum_fusion, s32[]{:T(128)} %bitcast.47, s32[16]{0:T(128)S(1)} %iota_add_fusion.1), kind=kOutput, calls=%fused_computation.7 | convolution fusion | flops 41945600 | bytes 4718660 | tf_op jit(solution)/shard_map/sb,sqr->bqr/dot_general | solution.py:77
  76.5 0.0 copy-done.2
  76.5 4.2 %fusion.22 = bf16[16,32,1024]{2,1,0:T(8,128)(2,1)S(1)} fusion(f32[16,32,1024]{2,0,1:T(8,128)S(1)} %fusion, f32[16,32,1024]{2,0,1:T(8,128)S(1)} %fusion.2, f32[32,16,1024]{2,0,1:T(8,128)S(1)} %copy-done.1, f32[16,32,1024]{2,1,0:T(8,128)S(1)} %copy-done.2, f32[16,32,1024]{2,1,0:T(8,128)S(1)} %reshape.195, bf16[16,32,1024]{2,1,0:T(8,128)(2,1)S(1)} %fusion.11, ...), kind=kOutput, calls=%fused_computation.34 | convolution fusion | flops 53745920 | bytes 13041676 | tf_op jit(solution)/shard_map/asr,sk->akr/dot_general | solution.py:142
  80.8 0.6 copy.25
  81.4 11.4 %all_to_all.18 = bf16[16,32,1024]{2,0,1:T(8,128)(2,1)S(1)} all-to-all(bf16[16,32,1024]{2,0,1:T(8,128)(2,1)S(1)} %copy.25), channel_id=1, replica_groups=mesh['az'=128,'rd'=2] {'rd'}, dimensions={1} | all-to-all | bytes 2097152 | tf_op jit(solution)/shard_map/all_to_all | solution.py:151
  92.8 1.1 %copy.26 = bf16[16,16,2,1024]{3,2,1,0:T(2,128)(2,1)S(1)} copy(bf16[16,16,2,1024]{3,0,1,2:T(8,128)(2,1)S(1)} %bitcast.152) | data formatting | bytes 2097152 | tf_op jit(solution)/shard_map/all_to_all | solution.py:151
  93.9 1.6 %all_to_all.16 = bf16[16,16,2048]{2,1,0:T(8,128)(2,1)} reshape(bf16[16,16,2,1024]{3,2,1,0:T(2,128)(2,1)S(1)} %copy.26) | data formatting | bytes 2097152 | tf_op jit(solution)/shard_map/all_to_all | solution.py:151
  (35 shorter events, 0.3 us)
Async XLA Ops:
  3.1 5.0 %copy-start = (f32[2,16,32,1024]{3,2,1,0:T(8,128)}, f32[2,16,32,1024]{3,2,1,0:T(8,128)S(1)}, u32[]{:S(2)}) copy-start(f32[2,16,32,1024]{3,2,1,0:T(8,128)S(1)} %convolution_bitcast_fusion) | copy-start | bytes 12582916
  3.8 10.8 %collective-permute-start.1 = (f32[2,32,1024]{2,1,0:T(8,128)S(1)}, f32[2,32,1024]{2,1,0:T(8,128)S(1)}, u32[]{:S(2)}, u32[]{:S(2)}) collective-permute-start(f32[2,32,1024]{2,1,0:T(8,128)S(1)} %get-tuple-element.6), channel_id=1, source_target_pairs={{2,0},{4,2},{6,4},{8,6},{10,8},{12,10},{14,12},{16,14},{18,16},{20... | collective-permute-start | bytes 786440 | tf_op jit(solution)/shard_map/ppermute | solution.py:24
  7.1 1.6 %copy-start.6 = (f32[5]{0:T(128)S(1)}, f32[5]{0:T(128)}, u32[]{:S(2)}) copy-start(f32[5]{0:T(128)} %param.7) | copy-start | bytes 64
  7.1 2.2 %copy-start.7 = (s32[6]{0:T(128)S(1)}, s32[6]{0:T(128)}, u32[]{:S(2)}) copy-start(s32[6]{0:T(128)} %param.9) | copy-start | bytes 76
  7.1 2.8 %copy-start.8 = (s32[16,16]{1,0:T(8,128)S(1)}, s32[16,16]{1,0:T(8,128)}, u32[]{:S(2)}) copy-start(s32[16,16]{1,0:T(8,128)} %param.8) | copy-start | bytes 3076
  7.1 9.5 %collective-permute-start = (f32[2,32,1024]{2,1,0:T(8,128)S(1)}, f32[2,32,1024]{2,1,0:T(8,128)S(1)}, u32[]{:S(2)}, u32[]{:S(2)}) collective-permute-start(f32[2,32,1024]{2,1,0:T(8,128)S(1)} %get-tuple-element.5), channel_id=1, source_target_pairs={{0,2},{2,4},{4,6},{6,8},{8,10},{10,12},{12,14},{14,16},{16,18},{18... | collective-permute-start | bytes 786440 | tf_op jit(solution)/shard_map/ppermute | solution.py:22
  16.6 0.7 copy-start.3
  24.7 42.4 %collective-permute-start.5 = (bf16[12,32,1024]{2,1,0:T(8,128)(2,1)}, bf16[12,32,1024]{2,1,0:T(8,128)(2,1)}, u32[]{:S(2)}, u32[]{:S(2)}) collective-permute-start(bf16[12,32,1024]{2,1,0:T(8,128)(2,1)} %get-tuple-element.12), channel_id=1, source_target_pairs={{2,0},{4,2},{6,4},{8,6},{10,8},{12,10},{14,12},{16,14},{18,16},{20... | collective-permute-start | bytes 2359304 | tf_op jit(solution)/shard_map/ppermute | solution.py:24
  35.3 31.9 %collective-permute-start.4 = (bf16[12,32,1024]{2,1,0:T(8,128)(2,1)}, bf16[12,32,1024]{2,1,0:T(8,128)(2,1)}, u32[]{:S(2)}, u32[]{:S(2)}) collective-permute-start(bf16[12,32,1024]{2,1,0:T(8,128)(2,1)} %get-tuple-element.11), channel_id=1, source_target_pairs={{0,2},{2,4},{4,6},{6,8},{8,10},{10,12},{12,14},{14,16},{16,18},{18... | collective-permute-start | bytes 2359304 | tf_op jit(solution)/shard_map/ppermute | solution.py:22
  35.3 17.4 %collective-permute-start.2 = (bf16[16,32,24]{2,1,0:T(8,128)(2,1)S(1)}, bf16[16,32,24]{2,1,0:T(8,128)(2,1)S(1)}, u32[]{:S(2)}, u32[]{:S(2)}) collective-permute-start(bf16[16,32,24]{2,1,0:T(8,128)(2,1)S(1)} %get-tuple-element.8), channel_id=1, source_target_pairs={{0,1},{2,3},{4,5},{6,7},{8,9},{10,11},{12,13},{14,15},{16,17},{18,... | collective-permute-start | bytes 73736 | tf_op jit(solution)/shard_map/ppermute | solution.py:22
  37.5 16.3 %collective-permute-start.3 = (bf16[16,32,24]{2,1,0:T(8,128)(2,1)S(1)}, bf16[16,32,24]{2,1,0:T(8,128)(2,1)S(1)}, u32[]{:S(2)}, u32[]{:S(2)}) collective-permute-start(bf16[16,32,24]{2,1,0:T(8,128)(2,1)S(1)} %get-tuple-element.7), channel_id=1, source_target_pairs={{1,0},{3,2},{5,4},{7,6},{9,8},{11,10},{13,12},{15,14},{17,16},{19,... | collective-permute-start | bytes 73736 | tf_op jit(solution)/shard_map/ppermute | solution.py:24
  72.6 3.9 %copy-start.1 = (f32[32,16,1024]{2,0,1:T(8,128)S(1)}, f32[32,16,1024]{2,0,1:T(8,128)}, u32[]{:S(2)}) copy-start(f32[32,16,1024]{2,0,1:T(8,128)} %fusion.30) | copy-start | bytes 6291460
  72.6 3.9 %copy-start.2 = (f32[16,32,1024]{2,1,0:T(8,128)S(1)}, f32[16,32,1024]{2,1,0:T(8,128)}, u32[]{:S(2)}) copy-start(f32[16,32,1024]{2,1,0:T(8,128)} %reshape.196) | copy-start | bytes 6291460
  72.6 3.9 %copy-start.4 = (f32[16,1024]{1,0:T(8,128)S(1)}, f32[16,1024]{1,0:T(8,128)}, u32[]{:S(2)}) copy-start(f32[16,1024]{1,0:T(8,128)} %get-tuple-element.30) | copy-start | bytes 196612
  72.6 3.9 %copy-start.5 = (f32[16,1024]{1,0:T(8,128)S(1)}, f32[16,1024]{1,0:T(8,128)}, u32[]{:S(2)}) copy-start(f32[16,1024]{1,0:T(8,128)} %get-tuple-element.31) | copy-start | bytes 196612
where the time goes:
time: 95.9 us; the launch traced here: 95.5 us
  matrix products  25.4 us (26%)
  starting transfers between devices  18.6 us (19%)
  waiting for transfers between devices  14.2 us (15%)
  local copies, waits for them, and re-layouts  14.1 us (15%)
  blocking collectives  11.4 us (12%)
  other arithmetic  9.52 us (10%)
  between operations  2.24 us (2%)
    ppermute x3, starting transfers between devices, with_halo(): lax.ppermute(head, axis, [((i + 1) % count, i) for i in range(ends)])  15.3 us
    ppermute x3, waiting for transfers between devices, with_halo(): lax.ppermute(tail, axis, [(i, (i + 1) % count) for i in range(ends)])  13.1 us
    all_to_all x1, blocking collectives, local(): lax.all_to_all(detection, 'rd', split_axis=1, concat_axis=2, tiled=True)  11.4 us
    dot_general x2, matrix products, range_mean(): jnp.einsum('aqbs,sr->aqbr', value_blocks, banded, preferred_element_type=...  6.59 us
    convert_element_type x1, other arithmetic, local(): log_power = jnp.log(integrated + 0.05).astype(jnp.bfloat16)  5.83 us
    reshape x2, local copies, waits for them, and re-layouts, range_mean(): sums = sums.reshape(dwells, local_bins, local_cells)  4.41 us
    dot_general x1, matrix products, local(): jnp.einsum('asr,sk->akr', circled, doppler_lag_band, preferred_element_ty...  4.25 us
    dot_general x1, matrix products, local(): jnp.einsum('sb,sqr->bqr', lead_band, log_power, preferred_element_type=jn...  3.89 us
  transfers between devices with their start and end apart: 6, of which 3 were waited for; matrix products, arithmetic and copies ran while one was open for 21% of the time, Pallas kernels for 0%

commit v1 on v0

v1 whole, which is shorter than its diff:
```python
import math

import jax
import jax.numpy as jnp
import numpy as np
from jax import lax
from jax.experimental import pallas as pl
from jax.experimental.pallas import tpu as pltpu
from jax.sharding import PartitionSpec as P

F32 = jnp.float32
BF16 = jnp.bfloat16
PULSES = 32
ROWS = 16
BINS = 16
LANES = 128
BLOCKS = 16
OWN = 8
CHUNKS = 4
PER = OWN // CHUNKS
WIDE = PER * LANES
REACH_R = 24
REACH_D = 4
REACH_A = 12
HALO = REACH_A + 2
SPAN = ROWS + 2 * REACH_A
ORDER = (0, 1, 2, 3, 12, 13, 14, 15, 4, 5, 6, 7, 8, 9, 10, 11)
EDGE = 8
KINDS = 10


def trig_table():
    bins = np.array([half * BINS + place for half in range(2) for place in ORDER])
    theta = 2.0 * np.pi * (np.outer(bins, np.arange(PULSES)) % PULSES) / PULSES
    cosines, sines = np.cos(theta), np.sin(theta)
    real = np.concatenate([cosines, sines], axis=1)
    imag = np.concatenate([-sines, cosines], axis=1)
    return np.concatenate([real, imag], axis=0).astype(np.float32)


def range_band():
    source = np.arange(3 * LANES)[:, None] - LANES
    lane = np.arange(LANES)[None, :]
    lead, lag = lane - source, source - lane
    bands = [((d > 1) & (d <= REACH_R)) for d in (lead, lag)]
    return np.concatenate(bands, axis=1).astype(np.float32)


def doppler_bands(group):
    tables = []
    for offsets in ((3, 4), (2,)):
        table = np.zeros((2, group, BINS, group * (BINS + EDGE)), np.float32)
        for side, sign in enumerate((-1, 1)):
            for row in range(group):
                for slot, place in enumerate(ORDER):
                    for offset in offsets:
                        source = (place + sign * offset) % PULSES
                        spot = ORDER.index(source % BINS)
                        if source < BINS:
                            column = row * BINS + spot
                        else:
                            column = group * BINS + row * EDGE + spot
                        table[side, row, slot, column] += 1.0
        tables.append(table.reshape(2 * group * BINS, -1))
    return tables


GROUP = 8


def kernel(
    echoes,
    taper,
    trig,
    band,
    dop_far,
    dop_near,
    beam,
    blank,
    cfar,
    out,
    held,
    power,
    off,
    off_edge,
    on,
    on_edge,
    logs,
    logs_edge,
    center,
    weighted,
    level,
    inverse,
    load_sem,
    send_sem,
    recv_sem,
):
    az, rd = lax.axis_index("az"), lax.axis_index("rd")
    count = lax.axis_size("az")
    odd = lax.rem(az, 2)
    pair = (az, 1 - rd)
    outer = (lax.rem(az - 1 + 2 * odd + count, count), 1 - rd)
    inner = (az + 1 - 2 * odd, rd)

    def physical(row):
        return row + odd * (ROWS - 1 - 2 * row)

    loads = []
    for c in range(CHUNKS):
        load = pltpu.make_async_copy(
            echoes.at[:, :, :, pl.ds(c * WIDE, WIDE)], held.at[c], load_sem.at[c]
        )
        load.start()
        loads.append(load)

    barrier = pltpu.get_barrier_semaphore()
    for target in (pair, outer, inner):
        pl.semaphore_signal(
            barrier, inc=1, device_id=target, device_id_type=pl.DeviceIdType.MESH
        )

    def transfer(c, kind, half):
        blocks = pl.ds(half * OWN + c * PER, PER)
        what = kind if kind < 2 else (kind - 2) % 4 + 2
        if what == 0:
            src, dst, target = power.at[0, blocks], power.at[1, blocks], pair
        elif what == 1:
            src, dst, target = power.at[1, blocks], power.at[0, blocks], pair
        elif what == 2:
            src, dst, target = power.at[1, blocks, pl.ds(0, HALO)], off.at[blocks], outer
        elif what == 3:
            src = power.at[0, blocks, pl.ds(0, 2), pl.ds(0, EDGE)]
            dst, target = off_edge.at[blocks], outer
        elif what == 4:
            src = power.at[0, blocks, pl.ds(ROWS - HALO, HALO)]
            dst, target = on.at[blocks], inner
        else:
            src = power.at[1, blocks, pl.ds(ROWS - 2, 2), pl.ds(0, EDGE)]
            dst, target = on_edge.at[blocks], inner
        return pltpu.make_async_remote_copy(
            src_ref=src,
            dst_ref=dst,
            send_sem=send_sem.at[c, kind],
            recv_sem=recv_sem.at[c, kind],
            device_id=target,
            device_id_type=pl.DeviceIdType.MESH,
        )

    sent = []

    def send(c, kind):
        copy = transfer(c, kind, rd if kind < 6 else 1 - rd)
        copy.start()
        sent.append(copy)

    def receive(c, kind):
        half = 1 - rd if kind in (0, 1, 2, 3, 8, 9) else rd
        transfer(c, kind, half).wait_recv()

    lane_parity = lax.rem(lax.broadcasted_iota(jnp.int32, (1, PULSES), 1), 2)
    signs = 1.0 - (2 * rd * lane_parity).astype(F32)
    tapered = taper[...] * signs
    bank = (trig[...] * jnp.concatenate([tapered, tapered], axis=1)).astype(BF16)

    for c in range(CHUNKS):
        loads[c].wait()
        for row in range(ROWS):
            spot = physical(row)
            pulses = jnp.concatenate([held[c, 0, spot], held[c, 1, spot]], axis=0)
            spectrum = jnp.dot(bank, pulses, preferred_element_type=F32)
            real, imag = spectrum[:PULSES], spectrum[PULSES:]
            powers = (real * real + imag * imag).astype(BF16)
            for part in range(PER):
                for half in range(2):
                    power[half, rd * OWN + c * PER + part, row] = powers[
                        half * BINS : (half + 1) * BINS, part * LANES : (part + 1) * LANES
                    ]
        if c == 0:
            pl.semaphore_wait(barrier, 3)
        for kind in (0, 1, 2, 3, 4, 5):
            send(c, kind)

    beams = [
        (beam[j] + odd.astype(F32) * (beam[4 - j] - beam[j])) * (1.0 / PULSES)
        for j in range(5)
    ]
    near_d = (2 - cfar[2]).astype(F32)
    near_a = (2 - cfar[4]).astype(F32)
    ones = jnp.ones((8, LANES), F32)
    scale_d = 1.0 / (ones * cfar[3].astype(F32))
    scale_d = jnp.concatenate([scale_d, scale_d], axis=0)
    scale_a = 1.0 / (ones * cfar[5].astype(F32))
    scale_a = jnp.concatenate([scale_a, scale_a], axis=0)
    doppler = (dop_far[...].astype(F32) + near_d * dop_near[...].astype(F32)).astype(BF16)

    lanes = lax.broadcasted_iota(jnp.int32, (8, LANES), 1)
    window = REACH_R - 1
    lead_in = jnp.clip(lanes - 1, 0, window).astype(F32)
    lag_in = jnp.clip(LANES - 2 - lanes, 0, window).astype(F32)
    lead_out, lag_out = window - lead_in, window - lag_in

    def weight_of(row, b):
        return blank[physical(row), b].astype(F32)

    @pl.loop(0, ROWS)
    def _(row):
        weights = [weight_of(row, b) for b in range(BLOCKS)]
        for b in range(BLOCKS):
            lead, lag = weights[b] * lead_in, weights[b] * lag_in
            if b > 0:
                lead = lead + weights[b - 1] * lead_out
            if b < BLOCKS - 1:
                lag = lag + weights[b + 1] * lag_out
            inverse[0, b, row] = 1.0 / jnp.maximum(lead, 1.0)
            inverse[1, b, row] = 1.0 / jnp.maximum(lag, 1.0)

    for edge in (0, BLOCKS + 1):
        weighted[edge] = jnp.zeros((ROWS, BINS, LANES), BF16)

    def integrate(rows, put):
        held_rows = [rows(e) for e in range(4)]
        last = None
        for t in range(put.count):
            held_rows.append(rows(t + 4))
            total = beams[0] * held_rows[0]
            for j in range(1, 5):
                total = total + beams[j] * held_rows[j]
            put(t, jnp.log(total + 0.05))
            held_rows.pop(0)

    def level_block(b):
        def rows(e):
            if e < HALO:
                return off[b, HALO - 1 - e].astype(F32)
            if e < HALO + ROWS:
                return power[0, b, e - HALO].astype(F32)
            return on[b, 2 * HALO + ROWS - 1 - e].astype(F32)

        def put(t, value):
            logs[t] = value
            row = t - REACH_A
            if 0 <= row < ROWS:
                rounded = value.astype(BF16)
                center[b, row] = rounded
                weighted[b + 1, row] = (
                    rounded.astype(F32) * weight_of(row, b)
                ).astype(BF16)

        put.count = SPAN
        integrate(rows, put)

        def edge_rows(e):
            if e < 2:
                return off_edge[b, 1 - e].astype(F32)
            if e < 2 + ROWS:
                return power[1, b, e - 2, 0:EDGE].astype(F32)
            return on_edge[b, 1 - (e - 2 - ROWS)].astype(F32)

        waiting = []

        def put_edge(t, value):
            waiting.append(value)
            if t % 2 == 1:
                logs_edge[t // 2] = jnp.concatenate(waiting, axis=0).astype(BF16)
                waiting.clear()

        put_edge.count = ROWS
        integrate(edge_rows, put_edge)

        means = []
        for group in range(ROWS // GROUP):
            stacked = jnp.concatenate(
                [
                    center[b, group * GROUP : (group + 1) * GROUP].reshape(
                        GROUP * BINS, LANES
                    ),
                    logs_edge[group * GROUP // 2 : (group + 1) * GROUP // 2].reshape(
                        GROUP * EDGE, LANES
                    ),
                ],
                axis=0,
            )
            sums = jnp.dot(doppler, stacked, preferred_element_type=F32)
            size = GROUP * BINS
            means.append(jnp.maximum(sums[:size], sums[size:]))

        far = REACH_A - 2
        lead = logs[0]
        lag = logs[REACH_A + 3]
        for d in range(1, far):
            lead = lead + logs[d]
            lag = lag + logs[REACH_A + 3 + d]
        for row in range(ROWS):
            azimuth = jnp.maximum(
                lead + near_a * logs[row + far], lag + near_a * logs[row + REACH_A + 2]
            )
            local = row % GROUP
            mean = means[row // GROUP][local * BINS : (local + 1) * BINS]
            level[b, row] = jnp.maximum(azimuth * scale_a, mean * scale_d)
            if row < ROWS - 1:
                lead = lead + (logs[row + far] - logs[row])
                lag = lag + (logs[row + REACH_A + 3 + far] - logs[row + REACH_A + 3])

    low = lax.broadcasted_iota(jnp.int32, (8, LANES), 0) < 4

    def finish_block(b):
        stacked = jnp.concatenate(
            [weighted[b + i].reshape(ROWS * BINS, LANES) for i in range(3)], axis=1
        )
        sums = jnp.dot(stacked, band[...], preferred_element_type=F32)
        cells = pl.ds(pl.multiple_of(b * LANES, LANES), LANES)
        for row in range(ROWS):
            here = slice(row * BINS, (row + 1) * BINS)
            lead, lag = inverse[0, b, row], inverse[1, b, row]
            lead = sums[here, :LANES] * jnp.concatenate([lead, lead], axis=0)
            lag = sums[here, LANES:] * jnp.concatenate([lag, lag], axis=0)
            noise = jnp.maximum(jnp.maximum(lead, lag), level[b, row])
            excess = weight_of(row, b) * (center[b, row].astype(F32) - noise)
            first, second = excess[:8], pltpu.roll(excess[8:], 4, 0)
            ordered = jnp.concatenate(
                [jnp.where(low, first, second), jnp.where(low, second, first)], axis=0
            )
            out[physical(row), :, cells] = ordered.astype(BF16)

    def blocks_of(first, size, body):
        @pl.loop(0, 2 * size)
        def _(index):
            body(lax.div(index, size) * OWN + first + lax.rem(index, size))

    def process(c):
        for kind in (2, 3, 4, 5, 6, 7, 8, 9):
            receive(c, kind)
        blocks_of(c * PER, PER, level_block)
        if c == 0:
            finish_block(0)
        elif c < CHUNKS - 1:
            blocks_of(c * PER - 1, PER, finish_block)
        else:
            blocks_of(c * PER - 1, PER + 1, finish_block)
            finish_block(OWN)

    for c in range(CHUNKS):
        receive(c, 0)
        receive(c, 1)
        for kind in (6, 7, 8, 9):
            send(c, kind)
        if c > 0:
            process(c - 1)
    process(CHUNKS - 1)

    for copy in sent:
        copy.wait_send()


def local(echoes, pulse_taper, beam_weights, blanking, cfar_sizes):
    far, near = doppler_bands(GROUP)
    vmem = pl.BlockSpec(memory_space=pltpu.VMEM)
    smem = pl.BlockSpec(memory_space=pltpu.SMEM)
    return pl.pallas_call(
        kernel,
        out_shape=jax.ShapeDtypeStruct((ROWS, BINS, BLOCKS * LANES), BF16),
        in_specs=[pl.BlockSpec(memory_space=pl.ANY)] + [vmem] * 5 + [smem] * 3,
        out_specs=vmem,
        scratch_shapes=[
            pltpu.VMEM((CHUNKS, 2, ROWS, PULSES, WIDE), BF16),
            pltpu.VMEM((2, BLOCKS, ROWS, BINS, LANES), BF16),
            pltpu.VMEM((BLOCKS, HALO, BINS, LANES), BF16),
            pltpu.VMEM((BLOCKS, 2, EDGE, LANES), BF16),
            pltpu.VMEM((BLOCKS, HALO, BINS, LANES), BF16),
            pltpu.VMEM((BLOCKS, 2, EDGE, LANES), BF16),
            pltpu.VMEM((SPAN, BINS, LANES), F32),
            pltpu.VMEM((ROWS // 2, BINS, LANES), BF16),
            pltpu.VMEM((BLOCKS, ROWS, BINS, LANES), BF16),
            pltpu.VMEM((BLOCKS + 2, ROWS, BINS, LANES), BF16),
            pltpu.VMEM((BLOCKS, ROWS, BINS, LANES), F32),
            pltpu.VMEM((2, BLOCKS, ROWS, 8, LANES), F32),
            pltpu.SemaphoreType.DMA((CHUNKS,)),
            pltpu.SemaphoreType.DMA((CHUNKS, KINDS)),
            pltpu.SemaphoreType.DMA((CHUNKS, KINDS)),
        ],
        compiler_params=pltpu.CompilerParams(
            collective_id=0, has_side_effects=True, vmem_limit_bytes=48 << 20
        ),
    )(
        echoes,
        pulse_taper.reshape(1, PULSES),
        jnp.asarray(trig_table()),
        jnp.asarray(range_band(), BF16),
        jnp.asarray(far, BF16),
        jnp.asarray(near, BF16),
        beam_weights,
        blanking,
        cfar_sizes,
    )


def solution(mesh):
    in_specs = (P(None, "az", None, "rd"), P(), P(), P("az", None), P())
    out_specs = P("az", "rd", None)
    return jax.shard_map(local, mesh=mesh, in_specs=in_specs, out_specs=out_specs, check_vma=False)
```

time: 95.9 us -> 49.5 us (0.52)
  the two profiles are of different devices: /device:TPU:1 before, /device:TPU:2 now
where the time goes in v1:
time: 49.5 us; the launch traced here: 49.2 us
  Pallas kernels  40.4 us (82%)
  local copies, waits for them, and re-layouts  8.71 us (18%)
    pallas_call x1, Pallas kernels, local(): pl.pallas_call(kernel, out_shape=jax.ShapeDtypeStruct((ROWS, BINS, BLOCKS...  40.4 us
    unnamed x19, local copies, waits for them, and re-layouts  8.71 us

profile of v1, /device:TPU:2, one launch (start us, length us, event | category | flops | bytes accessed | tf_op | source)
XLA Modules:
  0.0 49.2 jit_solution(8941925045178459782)
XLA Ops:
  0.0 0.0 copy-start
  0.0 1.6 %copy-done = bf16[2,16,32,1024]{3,2,1,0:T(8,128)(2,1)S(1)} copy-done((bf16[2,16,32,1024]{3,2,1,0:T(8,128)(2,1)S(1)}, bf16[2,16,32,1024]{3,2,1,0:T(8,128)(2,1)}, u32[]{:S(2)}) %copy-start) | copy-done | bytes 2097176
  1.6 0.0 copy-start.1
  1.6 0.9 %copy-done.1 = bf16[384,256]{1,0:T(8,128)(2,1)S(1)} copy-done((bf16[384,256]{1,0:T(8,128)(2,1)S(1)}, bf16[384,256]{1,0:T(8,128)(2,1)}, u32[]{:S(2)}) %copy-start.1) | copy-done | bytes 196632
  2.5 0.0 copy-start.2
  2.5 0.9 %copy-done.2 = bf16[256,192]{1,0:T(8,128)(2,1)S(1)} copy-done((bf16[256,192]{1,0:T(8,128)(2,1)S(1)}, bf16[256,192]{1,0:T(8,128)(2,1)}, u32[]{:S(2)}) %copy-start.2) | copy-done | bytes 98328
  3.4 0.0 copy-start.3
  3.4 0.9 %copy-done.3 = bf16[256,192]{1,0:T(8,128)(2,1)S(1)} copy-done((bf16[256,192]{1,0:T(8,128)(2,1)S(1)}, bf16[256,192]{1,0:T(8,128)(2,1)}, u32[]{:S(2)}) %copy-start.3) | copy-done | bytes 98328
  4.3 0.0 copy-start.4
  4.3 0.8 %copy-done.4 = f32[64,64]{1,0:T(8,128)S(1)} copy-done((f32[64,64]{1,0:T(8,128)S(1)}, f32[64,64]{1,0:T(8,128)}, u32[]{:S(2)}) %copy-start.4) | copy-done | bytes 16408
  5.1 0.0 copy-start.5
  5.1 0.7 %copy-done.5 = s32[16,16]{1,0:T(8,128)S(1)} copy-done((s32[16,16]{1,0:T(8,128)S(1)}, s32[16,16]{1,0:T(8,128)}, u32[]{:S(2)}) %copy-start.5) | copy-done | bytes 1048
  5.8 0.0 copy-start.6
  5.8 0.7 %copy-done.6 = f32[32]{0:T(128)S(1)} copy-done((f32[32]{0:T(128)S(1)}, f32[32]{0:T(128)}, u32[]{:S(2)}) %copy-start.6) | copy-done | bytes 152
  6.4 0.0 copy-start.7
  6.4 0.7 %copy-done.7 = f32[5]{0:T(128)S(1)} copy-done((f32[5]{0:T(128)S(1)}, f32[5]{0:T(128)}, u32[]{:S(2)}) %copy-start.7) | copy-done | bytes 44
  7.1 0.0 copy-start.8
  7.1 0.7 %copy-done.8 = s32[6]{0:T(128)S(1)} copy-done((s32[6]{0:T(128)S(1)}, s32[6]{0:T(128)}, u32[]{:S(2)}) %copy-start.8) | copy-done | bytes 48
  7.8 40.4 %shard_map.91 = bf16[16,16,2048]{2,1,0:T(8,128)(2,1)S(1)} custom-call(bf16[2,16,32,1024]{3,2,1,0:T(8,128)(2,1)S(1)} %copy-done, f32[1,32]{1,0:T(1,128)S(1)} %bitcast.1, f32[64,64]{1,0:T(8,128)S(1)} %copy-done.4, bf16[384,256]{1,0:T(8,128)(2,1)S(1)} %copy-done.1, bf16[256,192]{1,0:T(8,128)(2,1)S(1)} %copy-done.3, bf16[256,192]{1,0:T(8,128)(2,1)S(1)} %copy-done.2, ...), custom_call_target="tpu_custom_call" | custom-call | tf_op jit(solution)/shard_map/pallas_call | solution.py:359
  48.2 1.0 %copy.11 = bf16[16,16,2048]{2,1,0:T(8,128)(2,1)} copy(bf16[16,16,2048]{2,1,0:T(8,128)(2,1)S(1)} %shard_map.91) | data formatting | bytes 2097152
Async XLA Ops:
  0.0 1.6 %copy-start = (bf16[2,16,32,1024]{3,2,1,0:T(8,128)(2,1)S(1)}, bf16[2,16,32,1024]{3,2,1,0:T(8,128)(2,1)}, u32[]{:S(2)}) copy-start(bf16[2,16,32,1024]{3,2,1,0:T(8,128)(2,1)} %echoes.1) | copy-start | bytes 6291460
  1.6 0.9 %copy-start.1 = (bf16[384,256]{1,0:T(8,128)(2,1)S(1)}, bf16[384,256]{1,0:T(8,128)(2,1)}, u32[]{:S(2)}) copy-start(bf16[384,256]{1,0:T(8,128)(2,1)} %constant.9.clone.band) | copy-start | bytes 589828
  2.5 0.9 %copy-start.2 = (bf16[256,192]{1,0:T(8,128)(2,1)S(1)}, bf16[256,192]{1,0:T(8,128)(2,1)}, u32[]{:S(2)}) copy-start(bf16[256,192]{1,0:T(8,128)(2,1)} %constant.11.clone.dop_near) | copy-start | bytes 294916
  3.4 0.9 %copy-start.3 = (bf16[256,192]{1,0:T(8,128)(2,1)S(1)}, bf16[256,192]{1,0:T(8,128)(2,1)}, u32[]{:S(2)}) copy-start(bf16[256,192]{1,0:T(8,128)(2,1)} %constant.10.clone.dop_far) | copy-start | bytes 294916
  4.3 0.8 %copy-start.4 = (f32[64,64]{1,0:T(8,128)S(1)}, f32[64,64]{1,0:T(8,128)}, u32[]{:S(2)}) copy-start(f32[64,64]{1,0:T(8,128)} %constant.8.clone.trig) | copy-start | bytes 49156
  5.1 0.7 %copy-start.5 = (s32[16,16]{1,0:T(8,128)S(1)}, s32[16,16]{1,0:T(8,128)}, u32[]{:S(2)}) copy-start(s32[16,16]{1,0:T(8,128)} %blank.1) | copy-start | bytes 3076
  5.8 0.7 %copy-start.6 = (f32[32]{0:T(128)S(1)}, f32[32]{0:T(128)}, u32[]{:S(2)}) copy-start(f32[32]{0:T(128)} %param.10) | copy-start | bytes 388
  6.4 0.7 %copy-start.7 = (f32[5]{0:T(128)S(1)}, f32[5]{0:T(128)}, u32[]{:S(2)}) copy-start(f32[5]{0:T(128)} %beam.1) | copy-start | bytes 64
  7.1 0.7 %copy-start.8 = (s32[6]{0:T(128)S(1)}, s32[6]{0:T(128)}, u32[]{:S(2)}) copy-start(s32[6]{0:T(128)} %cfar.1) | copy-start | bytes 76

commit v2 on v1

--- a/solution.py
+++ b/solution.py
@@ -70,6 +70,21 @@
 
 def kernel(
     echoes,
+    *refs,
+):
+    sources, (result, *scratch) = refs[:8], refs[8:]
+    tables, (stage_sem, *scratch) = scratch[:8], scratch[8:]
+    stages = []
+    for index, (source, table) in enumerate(zip(sources, tables)):
+        stage = pltpu.make_async_copy(source, table, stage_sem.at[index])
+        stages.append(stage)
+    body(echoes, result, stages, *tables, *scratch)
+
+
+def body(
+    echoes,
+    result,
+    stages,
     taper,
     trig,
     band,
@@ -94,6 +109,7 @@
     load_sem,
     send_sem,
     recv_sem,
+    out_sem,
 ):
     az, rd = lax.axis_index("az"), lax.axis_index("rd")
     count = lax.axis_size("az")
@@ -110,8 +126,13 @@
         load = pltpu.make_async_copy(
             echoes.at[:, :, :, pl.ds(c * WIDE, WIDE)], held.at[c], load_sem.at[c]
         )
+        loads.append(load)
+    for stage in stages[:2]:
+        stage.start()
+    for load in loads:
         load.start()
-        loads.append(load)
+    for stage in stages[2:]:
+        stage.start()
 
     barrier = pltpu.get_barrier_semaphore()
     for target in (pair, outer, inner):
@@ -157,6 +178,8 @@
         half = 1 - rd if kind in (0, 1, 2, 3, 8, 9) else rd
         transfer(c, kind, half).wait_recv()
 
+    for stage in stages[:2]:
+        stage.wait()
     lane_parity = lax.rem(lax.broadcasted_iota(jnp.int32, (1, PULSES), 1), 2)
     signs = 1.0 - (2 * rd * lane_parity).astype(F32)
     tapered = taper[...] * signs
@@ -180,6 +203,8 @@
         for kind in (0, 1, 2, 3, 4, 5):
             send(c, kind)
 
+    for stage in stages[2:]:
+        stage.wait()
     beams = [
         (beam[j] + odd.astype(F32) * (beam[4 - j] - beam[j])) * (1.0 / PULSES)
         for j in range(5)
@@ -303,12 +328,15 @@
 
     low = lax.broadcasted_iota(jnp.int32, (8, LANES), 0) < 4
 
+    def emit(b):
+        cells = pl.ds(pl.multiple_of(b * LANES, LANES), LANES)
+        return pltpu.make_async_copy(out.at[b], result.at[:, :, cells], out_sem.at[b])
+
     def finish_block(b):
         stacked = jnp.concatenate(
             [weighted[b + i].reshape(ROWS * BINS, LANES) for i in range(3)], axis=1
         )
         sums = jnp.dot(stacked, band[...], preferred_element_type=F32)
-        cells = pl.ds(pl.multiple_of(b * LANES, LANES), LANES)
         for row in range(ROWS):
             here = slice(row * BINS, (row + 1) * BINS)
             lead, lag = inverse[0, b, row], inverse[1, b, row]
@@ -320,7 +348,8 @@
             ordered = jnp.concatenate(
                 [jnp.where(low, first, second), jnp.where(low, second, first)], axis=0
             )
-            out[physical(row), :, cells] = ordered.astype(BF16)
+            out[b, physical(row)] = ordered.astype(BF16)
+        emit(b).start()
 
     def blocks_of(first, size, body):
         @pl.loop(0, 2 * size)
@@ -351,17 +380,30 @@
     for copy in sent:
         copy.wait_send()
 
+    @pl.loop(0, BLOCKS)
+    def _(b):
+        emit(b).wait()
+
 
 def local(echoes, pulse_taper, beam_weights, blanking, cfar_sizes):
     far, near = doppler_bands(GROUP)
-    vmem = pl.BlockSpec(memory_space=pltpu.VMEM)
-    smem = pl.BlockSpec(memory_space=pltpu.SMEM)
+    hbm = pl.BlockSpec(memory_space=pltpu.HBM)
     return pl.pallas_call(
         kernel,
         out_shape=jax.ShapeDtypeStruct((ROWS, BINS, BLOCKS * LANES), BF16),
-        in_specs=[pl.BlockSpec(memory_space=pl.ANY)] + [vmem] * 5 + [smem] * 3,
-        out_specs=vmem,
+        in_specs=[hbm] * 9,
+        out_specs=pl.BlockSpec(memory_space=pl.ANY),
         scratch_shapes=[
+            pltpu.VMEM((1, PULSES), F32),
+            pltpu.VMEM((2 * PULSES, 2 * PULSES), F32),
+            pltpu.VMEM((3 * LANES, 2 * LANES), BF16),
+            pltpu.VMEM((2 * GROUP * BINS, GROUP * (BINS + EDGE)), BF16),
+            pltpu.VMEM((2 * GROUP * BINS, GROUP * (BINS + EDGE)), BF16),
+            pltpu.SMEM((5,), F32),
+            pltpu.SMEM((ROWS, BLOCKS), jnp.int32),
+            pltpu.SMEM((6,), jnp.int32),
+            pltpu.SemaphoreType.DMA((8,)),
+            pltpu.VMEM((BLOCKS, ROWS, BINS, LANES), BF16),
             pltpu.VMEM((CHUNKS, 2, ROWS, PULSES, WIDE), BF16),
             pltpu.VMEM((2, BLOCKS, ROWS, BINS, LANES), BF16),
             pltpu.VMEM((BLOCKS, HALO, BINS, LANES), BF16),
@@ -377,9 +419,10 @@
             pltpu.SemaphoreType.DMA((CHUNKS,)),
             pltpu.SemaphoreType.DMA((CHUNKS, KINDS)),
             pltpu.SemaphoreType.DMA((CHUNKS, KINDS)),
+            pltpu.SemaphoreType.DMA((BLOCKS,)),
         ],
         compiler_params=pltpu.CompilerParams(
-            collective_id=0, has_side_effects=True, vmem_limit_bytes=48 << 20
+            collective_id=0, has_side_effects=True, vmem_limit_bytes=67043328
         ),
     )(
         echoes,

time: 49.5 us -> 43.7 us (0.88)
  local copies, waits for them, and re-layouts: 8.71 us -> 2.3 us
  Pallas kernels: 40.4 us -> 41.2 us
    unnamed x19 -> x1, local copies, waits for them, and re-layouts: 8.71 us -> 2.3 us
    pallas_call x1, Pallas kernels: 40.4 us -> 41.2 us  [local(): pl.pallas_call(kernel, out_shape=jax.ShapeDtypeStruct((ROWS, BINS, BLOCKS...]
where the time goes in v2:
time: 43.7 us; the launch traced here: 43.5 us
  Pallas kernels  41.2 us (94%)
  local copies, waits for them, and re-layouts  2.3 us (5%)
    pallas_call x1, Pallas kernels, local(): pl.pallas_call(kernel, out_shape=jax.ShapeDtypeStruct((ROWS, BINS, BLOCKS...  41.2 us
    unnamed x1, local copies, waits for them, and re-layouts  2.3 us

profile of v2, /device:TPU:2, one launch (start us, length us, event | category | flops | bytes accessed | tf_op | source)
XLA Modules:
  0.0 43.5 jit_solution(13183138510053634426)
XLA Ops:
  0.0 41.2 %shard_map.91 = bf16[16,16,2048]{2,1,0:T(8,128)(2,1)} custom-call(bf16[2,16,32,1024]{3,2,1,0:T(8,128)(2,1)} %echoes.1, f32[1,32]{1,0:T(1,128)} %bitcast.1, f32[64,64]{1,0:T(8,128)} %constant.8.clone.refs_1_, bf16[384,256]{1,0:T(8,128)(2,1)} %constant.9.clone.refs_2_, bf16[256,192]{1,0:T(8,128)(2,1)} %constant.10.clone.refs_3_, ...), custom_call_target="tpu_custom_call" | custom-call | tf_op jit(solution)/shard_map/pallas_call | solution.py:391
  41.2 2.3 %copy.11 = bf16[16,16,2048]{2,1,0:T(8,128)(2,1)} copy(bf16[16,16,2048]{2,1,0:T(8,128)(2,1)} %shard_map.91) | data formatting | bytes 2097152

commit v3 on v2

--- a/solution.py
+++ b/solution.py
@@ -26,7 +26,8 @@
 SPAN = ROWS + 2 * REACH_A
 ORDER = (0, 1, 2, 3, 12, 13, 14, 15, 4, 5, 6, 7, 8, 9, 10, 11)
 EDGE = 8
-KINDS = 10
+PIECES = ((0, 2), (2, 2), (4, 2), (6, 1), (7, 1))
+PAIR_KINDS, KINDS = 5, 13
 
 
 def trig_table():
@@ -121,10 +122,16 @@
     def physical(row):
         return row + odd * (ROWS - 1 - 2 * row)
 
+    def block_at(half, place):
+        return OWN - 1 - place + half * (1 + 2 * place)
+
     loads = []
     for c in range(CHUNKS):
+        first = (rd * c + (1 - rd) * (CHUNKS - 1 - c)) * WIDE
         load = pltpu.make_async_copy(
-            echoes.at[:, :, :, pl.ds(c * WIDE, WIDE)], held.at[c], load_sem.at[c]
+            echoes.at[:, :, :, pl.ds(pl.multiple_of(first, WIDE), WIDE)],
+            held.at[c],
+            load_sem.at[c],
         )
         loads.append(load)
     for stage in stages[:2]:
@@ -141,18 +148,25 @@
         )
 
     def transfer(c, kind, half):
-        blocks = pl.ds(half * OWN + c * PER, PER)
-        what = kind if kind < 2 else (kind - 2) % 4 + 2
-        if what == 0:
-            src, dst, target = power.at[0, blocks], power.at[1, blocks], pair
-        elif what == 1:
-            src, dst, target = power.at[1, blocks], power.at[0, blocks], pair
-        elif what == 2:
+        place, size = PIECES[c]
+        blocks = pl.ds(half * OWN + place, size)
+        what = kind if kind < PAIR_KINDS + 4 else kind - 4
+        if what < PAIR_KINDS:
+            bins, cut = (
+                (0, (pl.ds(0, HALO),)),
+                (0, (pl.ds(HALO, 2), pl.ds(0, EDGE))),
+                (1, (pl.ds(0, 2), pl.ds(0, EDGE))),
+                (1, (pl.ds(2, HALO),)),
+                (1, (pl.ds(0, 2), pl.ds(EDGE, EDGE))),
+            )[what]
+            src = power.at[(bins, blocks) + cut]
+            dst, target = power.at[(1 - bins, blocks) + cut], pair
+        elif what == 5:
             src, dst, target = power.at[1, blocks, pl.ds(0, HALO)], off.at[blocks], outer
-        elif what == 3:
+        elif what == 6:
             src = power.at[0, blocks, pl.ds(0, 2), pl.ds(0, EDGE)]
             dst, target = off_edge.at[blocks], outer
-        elif what == 4:
+        elif what == 7:
             src = power.at[0, blocks, pl.ds(ROWS - HALO, HALO)]
             dst, target = on.at[blocks], inner
         else:
@@ -169,14 +183,16 @@
 
     sent = []
 
-    def send(c, kind):
-        copy = transfer(c, kind, rd if kind < 6 else 1 - rd)
-        copy.start()
-        sent.append(copy)
-
-    def receive(c, kind):
-        half = 1 - rd if kind in (0, 1, 2, 3, 8, 9) else rd
-        transfer(c, kind, half).wait_recv()
+    def send(c, *kinds):
+        for kind in kinds:
+            copy = transfer(c, kind, rd if kind < PAIR_KINDS + 4 else 1 - rd)
+            copy.start()
+            sent.append(copy)
+
+    def receive(c, *kinds):
+        for kind in kinds:
+            other = kind < PAIR_KINDS + 2 or kind > PAIR_KINDS + 5
+            transfer(c, kind, 1 - rd if other else rd).wait_recv()
 
     for stage in stages[:2]:
         stage.wait()
@@ -194,14 +210,18 @@
             real, imag = spectrum[:PULSES], spectrum[PULSES:]
             powers = (real * real + imag * imag).astype(BF16)
             for part in range(PER):
+                place = c * PER + part * rd + (PER - 1 - part) * (1 - rd)
                 for half in range(2):
-                    power[half, rd * OWN + c * PER + part, row] = powers[
+                    power[half, rd * OWN + place, row] = powers[
                         half * BINS : (half + 1) * BINS, part * LANES : (part + 1) * LANES
                     ]
         if c == 0:
             pl.semaphore_wait(barrier, 3)
-        for kind in (0, 1, 2, 3, 4, 5):
-            send(c, kind)
+        for piece, (place, _) in enumerate(PIECES):
+            if place // PER == c:
+                send(piece, 0, 1, 2, 5, 6, 7, 8)
+    for piece in range(len(PIECES)):
+        send(piece, 3, 4)
 
     for stage in stages[2:]:
         stage.wait()
@@ -253,13 +273,15 @@
             put(t, jnp.log(total + 0.05))
             held_rows.pop(0)
 
-    def level_block(b):
+    def level_block(half, place):
+        b, q = block_at(half, place), half * OWN + place
+
         def rows(e):
             if e < HALO:
-                return off[b, HALO - 1 - e].astype(F32)
+                return off[q, HALO - 1 - e].astype(F32)
             if e < HALO + ROWS:
-                return power[0, b, e - HALO].astype(F32)
-            return on[b, 2 * HALO + ROWS - 1 - e].astype(F32)
+                return power[0, q, e - HALO].astype(F32)
+            return on[q, 2 * HALO + ROWS - 1 - e].astype(F32)
 
         def put(t, value):
             logs[t] = value
@@ -276,10 +298,10 @@
 
         def edge_rows(e):
             if e < 2:
-                return off_edge[b, 1 - e].astype(F32)
+                return off_edge[q, 1 - e].astype(F32)
             if e < 2 + ROWS:
-                return power[1, b, e - 2, 0:EDGE].astype(F32)
-            return on_edge[b, 1 - (e - 2 - ROWS)].astype(F32)
+                return power[1, q, e - 2, 0:EDGE].astype(F32)
+            return on_edge[q, 1 - (e - 2 - ROWS)].astype(F32)
 
         waiting = []
 
@@ -351,31 +373,31 @@
             out[b, physical(row)] = ordered.astype(BF16)
         emit(b).start()
 
-    def blocks_of(first, size, body):
+    def levels(c, half):
+        place, size = PIECES[c]
+
+        @pl.loop(0, size)
+        def _(index):
+            level_block(half, place + index)
+
+    def finishes(first, size):
         @pl.loop(0, 2 * size)
         def _(index):
-            body(lax.div(index, size) * OWN + first + lax.rem(index, size))
-
-    def process(c):
-        for kind in (2, 3, 4, 5, 6, 7, 8, 9):
-            receive(c, kind)
-        blocks_of(c * PER, PER, level_block)
-        if c == 0:
-            finish_block(0)
-        elif c < CHUNKS - 1:
-            blocks_of(c * PER - 1, PER, finish_block)
-        else:
-            blocks_of(c * PER - 1, PER + 1, finish_block)
-            finish_block(OWN)
-
-    for c in range(CHUNKS):
-        receive(c, 0)
-        receive(c, 1)
-        for kind in (6, 7, 8, 9):
-            send(c, kind)
-        if c > 0:
-            process(c - 1)
-    process(CHUNKS - 1)
+            finish_block(block_at(lax.div(index, size), first + lax.rem(index, size)))
+
+    for c in range(len(PIECES)):
+        receive(c, 0, 1, 2)
+        send(c, 9, 10)
+    for c, (place, size) in enumerate(PIECES):
+        receive(c, 3, 4)
+        send(c, 11, 12)
+        receive(c, 9, 10, 7, 8)
+        levels(c, rd)
+        receive(c, 11, 12, 5, 6)
+        levels(c, 1 - rd)
+        first = max(place - 1, 0)
+        last = place + size - (c < len(PIECES) - 1)
+        finishes(first, last - first)
 
     for copy in sent:
         copy.wait_send()
@@ -417,14 +439,15 @@
             pltpu.VMEM((BLOCKS, ROWS, BINS, LANES), F32),
             pltpu.VMEM((2, BLOCKS, ROWS, 8, LANES), F32),
             pltpu.SemaphoreType.DMA((CHUNKS,)),
-            pltpu.SemaphoreType.DMA((CHUNKS, KINDS)),
-            pltpu.SemaphoreType.DMA((CHUNKS, KINDS)),
+            pltpu.SemaphoreType.DMA((len(PIECES), KINDS)),
+            pltpu.SemaphoreType.DMA((len(PIECES), KINDS)),
             pltpu.SemaphoreType.DMA((BLOCKS,)),
         ],
         compiler_params=pltpu.CompilerParams(
-            collective_id=0, has_side_effects=True, vmem_limit_bytes=67043328
+            collective_id=0, has_side_effects=True, vmem_limit_bytes=48<<20
         ),
     )(
+        *(pltpu.with_memory_space_constraint(x, pltpu.HBM) for x in (
         echoes,
         pulse_taper.reshape(1, PULSES),
         jnp.asarray(trig_table()),
@@ -434,6 +457,7 @@
         beam_weights,
         blanking,
         cfar_sizes,
+        ))
     )
 
 

time: 43.7 us -> 37.9 us (0.87)
  the two profiles are of different devices: /device:TPU:2 before, /device:TPU:1 now
where the time goes in v3:
time: 37.9 us; the launch traced here: 37.8 us
  Pallas kernels  36.9 us (97%)
  local copies, waits for them, and re-layouts  0.97 us (3%)
    pallas_call x1, Pallas kernels, local(): pl.pallas_call(kernel, out_shape=jax.ShapeDtypeStruct((ROWS, BINS, BLOCKS...  36.9 us
    unnamed x1, local copies, waits for them, and re-layouts  0.97 us

profile of v3, /device:TPU:1, one launch (start us, length us, event | category | flops | bytes accessed | tf_op | source)
XLA Modules:
  0.0 37.8 jit_solution(1197014315439971642)
XLA Ops:
  0.0 36.9 %shard_map.91 = bf16[16,16,2048]{2,1,0:T(8,128)(2,1)S(1)} custom-call(bf16[2,16,32,1024]{3,2,1,0:T(8,128)(2,1)} %echoes.1, f32[1,32]{1,0:T(1,128)} %bitcast.1, f32[64,64]{1,0:T(8,128)} %constant.8.clone.refs_1_, bf16[384,256]{1,0:T(8,128)(2,1)} %constant.9.clone.refs_2_, bf16[256,192]{1,0:T(8,128)(2,1)} %constant.10.clone.refs_3_, ...), custom_call_target="tpu_custom_call" | custom-call | tf_op jit(solution)/shard_map/pallas_call | solution.py:413
  36.9 1.0 %copy.11 = bf16[16,16,2048]{2,1,0:T(8,128)(2,1)} copy(bf16[16,16,2048]{2,1,0:T(8,128)(2,1)S(1)} %shard_map.91) | data formatting | bytes 2097152

commit v4 on v3

--- a/solution.py
+++ b/solution.py
@@ -27,6 +27,7 @@
 ORDER = (0, 1, 2, 3, 12, 13, 14, 15, 4, 5, 6, 7, 8, 9, 10, 11)
 EDGE = 8
 PIECES = ((0, 2), (2, 2), (4, 2), (6, 1), (7, 1))
+AHEAD = 2
 PAIR_KINDS, KINDS = 5, 13
 
 
@@ -94,7 +95,6 @@
     beam,
     blank,
     cfar,
-    out,
     held,
     power,
     off,
@@ -110,7 +110,6 @@
     load_sem,
     send_sem,
     recv_sem,
-    out_sem,
 ):
     az, rd = lax.axis_index("az"), lax.axis_index("rd")
     count = lax.axis_size("az")
@@ -181,13 +180,11 @@
             device_id_type=pl.DeviceIdType.MESH,
         )
 
-    sent = []
+    urgent = az == count - 1
 
     def send(c, *kinds):
         for kind in kinds:
-            copy = transfer(c, kind, rd if kind < PAIR_KINDS + 4 else 1 - rd)
-            copy.start()
-            sent.append(copy)
+            transfer(c, kind, rd if kind < PAIR_KINDS + 4 else 1 - rd).start()
 
     def receive(c, *kinds):
         for kind in kinds:
@@ -219,9 +216,31 @@
             pl.semaphore_wait(barrier, 3)
         for piece, (place, _) in enumerate(PIECES):
             if place // PER == c:
-                send(piece, 0, 1, 2, 5, 6, 7, 8)
-    for piece in range(len(PIECES)):
-        send(piece, 3, 4)
+                send(piece, 0, 1, 2, 7, 8)
+
+                if piece < AHEAD:
+                    send(piece, 5, 6)
+                else:
+
+                    @pl.when(urgent)
+                    def _():
+                        send(piece, 5, 6)
+
+                if piece > 0:
+
+                    @pl.when(jnp.logical_not(urgent))
+                    def _():
+                        send(piece - 1, 3, 4)
+
+    @pl.when(jnp.logical_not(urgent))
+    def _():
+        send(len(PIECES) - 1, 3, 4)
+
+    @pl.when(urgent)
+    def _():
+        for piece in range(len(PIECES)):
+            send(piece, 3, 4)
+
 
     for stage in stages[2:]:
         stage.wait()
@@ -350,11 +369,8 @@
 
     low = lax.broadcasted_iota(jnp.int32, (8, LANES), 0) < 4
 
-    def emit(b):
+    def finish_block(b):
         cells = pl.ds(pl.multiple_of(b * LANES, LANES), LANES)
-        return pltpu.make_async_copy(out.at[b], result.at[:, :, cells], out_sem.at[b])
-
-    def finish_block(b):
         stacked = jnp.concatenate(
             [weighted[b + i].reshape(ROWS * BINS, LANES) for i in range(3)], axis=1
         )
@@ -370,8 +386,7 @@
             ordered = jnp.concatenate(
                 [jnp.where(low, first, second), jnp.where(low, second, first)], axis=0
             )
-            out[b, physical(row)] = ordered.astype(BF16)
-        emit(b).start()
+            result[physical(row), :, cells] = ordered.astype(BF16)
 
     def levels(c, half):
         place, size = PIECES[c]
@@ -381,30 +396,48 @@
             level_block(half, place + index)
 
     def finishes(first, size):
-        @pl.loop(0, 2 * size)
+        @pl.loop(0, size)
         def _(index):
-            finish_block(block_at(lax.div(index, size), first + lax.rem(index, size)))
-
-    for c in range(len(PIECES)):
-        receive(c, 0, 1, 2)
-        send(c, 9, 10)
+            finish_block(block_at(0, first + index))
+            finish_block(block_at(1, first + index))
+
+    def relay(c):
+        if c < len(PIECES):
+            receive(c, 0, 1, 2)
+            send(c, 9, 10)
+        if c + AHEAD < len(PIECES):
+
+            @pl.when(jnp.logical_not(urgent))
+            def _():
+                send(c + AHEAD, 5, 6)
+
+    for c in range(AHEAD):
+        relay(c)
+
+    @pl.when(urgent)
+    def _():
+        for c in range(AHEAD, len(PIECES)):
+            relay(c)
+
     for c, (place, size) in enumerate(PIECES):
         receive(c, 3, 4)
         send(c, 11, 12)
         receive(c, 9, 10, 7, 8)
         levels(c, rd)
+
+        @pl.when(jnp.logical_not(urgent))
+        def _():
+            relay(c + AHEAD)
+
         receive(c, 11, 12, 5, 6)
         levels(c, 1 - rd)
         first = max(place - 1, 0)
         last = place + size - (c < len(PIECES) - 1)
         finishes(first, last - first)
 
-    for copy in sent:
-        copy.wait_send()
-
-    @pl.loop(0, BLOCKS)
-    def _(b):
-        emit(b).wait()
+    for c in range(len(PIECES)):
+        for kind in range(KINDS):
+            transfer(c, kind, rd if kind < PAIR_KINDS + 4 else 1 - rd).wait_send()
 
 
 def local(echoes, pulse_taper, beam_weights, blanking, cfar_sizes):
@@ -414,7 +447,7 @@
         kernel,
         out_shape=jax.ShapeDtypeStruct((ROWS, BINS, BLOCKS * LANES), BF16),
         in_specs=[hbm] * 9,
-        out_specs=pl.BlockSpec(memory_space=pl.ANY),
+        out_specs=pl.BlockSpec(memory_space=pltpu.VMEM),
         scratch_shapes=[
             pltpu.VMEM((1, PULSES), F32),
             pltpu.VMEM((2 * PULSES, 2 * PULSES), F32),
@@ -425,7 +458,6 @@
             pltpu.SMEM((ROWS, BLOCKS), jnp.int32),
             pltpu.SMEM((6,), jnp.int32),
             pltpu.SemaphoreType.DMA((8,)),
-            pltpu.VMEM((BLOCKS, ROWS, BINS, LANES), BF16),
             pltpu.VMEM((CHUNKS, 2, ROWS, PULSES, WIDE), BF16),
             pltpu.VMEM((2, BLOCKS, ROWS, BINS, LANES), BF16),
             pltpu.VMEM((BLOCKS, HALO, BINS, LANES), BF16),
@@ -441,7 +473,6 @@
             pltpu.SemaphoreType.DMA((CHUNKS,)),
             pltpu.SemaphoreType.DMA((len(PIECES), KINDS)),
             pltpu.SemaphoreType.DMA((len(PIECES), KINDS)),
-            pltpu.SemaphoreType.DMA((BLOCKS,)),
         ],
         compiler_params=pltpu.CompilerParams(
             collective_id=0, has_side_effects=True, vmem_limit_bytes=48<<20

time: 37.9 us -> 35 us (0.923)
  the two profiles are of different devices: /device:TPU:1 before, /device:TPU:25 now
where the time goes in v4:
time: 35 us; the launch traced here: 34.9 us
  Pallas kernels  33.9 us (97%)
  local copies, waits for them, and re-layouts  0.97 us (3%)
    pallas_call x1, Pallas kernels, local(): pl.pallas_call(kernel, out_shape=jax.ShapeDtypeStruct((ROWS, BINS, BLOCKS...  33.9 us
    unnamed x1, local copies, waits for them, and re-layouts  0.97 us

profile of v4, /device:TPU:25, one launch (start us, length us, event | category | flops | bytes accessed | tf_op | source)
XLA Modules:
  0.0 34.9 jit_solution(3814840030628030842)
XLA Ops:
  0.0 33.9 %shard_map.91 = bf16[16,16,2048]{2,1,0:T(8,128)(2,1)S(1)} custom-call(bf16[2,16,32,1024]{3,2,1,0:T(8,128)(2,1)} %echoes.1, f32[1,32]{1,0:T(1,128)} %bitcast.1, f32[64,64]{1,0:T(8,128)} %constant.8.clone.refs_1_, bf16[384,256]{1,0:T(8,128)(2,1)} %constant.9.clone.refs_2_, bf16[256,192]{1,0:T(8,128)(2,1)} %constant.10.clone.refs_3_, ...), custom_call_target="tpu_custom_call" | custom-call | tf_op jit(solution)/shard_map/pallas_call | solution.py:446
  33.9 1.0 %copy.11 = bf16[16,16,2048]{2,1,0:T(8,128)(2,1)} copy(bf16[16,16,2048]{2,1,0:T(8,128)(2,1)S(1)} %shard_map.91) | data formatting | bytes 2097152

commit v5 on v4

--- a/solution.py
+++ b/solution.py
@@ -395,11 +395,11 @@
         def _(index):
             level_block(half, place + index)
 
-    def finishes(first, size):
-        @pl.loop(0, size)
-        def _(index):
-            finish_block(block_at(0, first + index))
-            finish_block(block_at(1, first + index))
+    def finishes(c, half):
+        place, size = PIECES[c]
+        last = place + size - (c < len(PIECES) - 1)
+        for each in range(max(place - 1, 0), last):
+            finish_block(block_at(half, each))
 
     def relay(c):
         if c < len(PIECES):
@@ -419,11 +419,13 @@
         for c in range(AHEAD, len(PIECES)):
             relay(c)
 
-    for c, (place, size) in enumerate(PIECES):
+    for c in range(len(PIECES)):
         receive(c, 3, 4)
         send(c, 11, 12)
         receive(c, 9, 10, 7, 8)
         levels(c, rd)
+        if c > 0:
+            finishes(c, rd)
 
         @pl.when(jnp.logical_not(urgent))
         def _():
@@ -431,9 +433,9 @@
 
         receive(c, 11, 12, 5, 6)
         levels(c, 1 - rd)
-        first = max(place - 1, 0)
-        last = place + size - (c < len(PIECES) - 1)
-        finishes(first, last - first)
+        if c == 0:
+            finishes(c, rd)
+        finishes(c, 1 - rd)
 
     for c in range(len(PIECES)):
         for kind in range(KINDS):

time: 35 us -> 34.3 us (0.980)
  Pallas kernels: 33.9 us -> 33.3 us
    pallas_call x1, Pallas kernels: 33.9 us -> 33.3 us  [local(): pl.pallas_call(kernel, out_shape=jax.ShapeDtypeStruct((ROWS, BINS, BLOCKS...]
where the time goes in v5:
time: 34.3 us; the launch traced here: 34.2 us
  Pallas kernels  33.3 us (97%)
  local copies, waits for them, and re-layouts  0.97 us (3%)
    pallas_call x1, Pallas kernels, local(): pl.pallas_call(kernel, out_shape=jax.ShapeDtypeStruct((ROWS, BINS, BLOCKS...  33.3 us
    unnamed x1, local copies, waits for them, and re-layouts  0.97 us

profile of v5, /device:TPU:25, one launch (start us, length us, event | category | flops | bytes accessed | tf_op | source)
XLA Modules:
  0.0 34.2 jit_solution(8523804296333077522)
XLA Ops:
  0.0 33.3 %shard_map.91 = bf16[16,16,2048]{2,1,0:T(8,128)(2,1)S(1)} custom-call(bf16[2,16,32,1024]{3,2,1,0:T(8,128)(2,1)} %echoes.1, f32[1,32]{1,0:T(1,128)} %bitcast.1, f32[64,64]{1,0:T(8,128)} %constant.8.clone.refs_1_, bf16[384,256]{1,0:T(8,128)(2,1)} %constant.9.clone.refs_2_, bf16[256,192]{1,0:T(8,128)(2,1)} %constant.10.clone.refs_3_, ...), custom_call_target="tpu_custom_call" | custom-call | tf_op jit(solution)/shard_map/pallas_call | solution.py:448
  33.3 1.0 %copy.11 = bf16[16,16,2048]{2,1,0:T(8,128)(2,1)} copy(bf16[16,16,2048]{2,1,0:T(8,128)(2,1)S(1)} %shard_map.91) | data formatting | bytes 2097152

commit v6 on v5

--- a/solution.py
+++ b/solution.py
@@ -281,10 +281,9 @@
     for edge in (0, BLOCKS + 1):
         weighted[edge] = jnp.zeros((ROWS, BINS, LANES), BF16)
 
-    def integrate(rows, put):
-        held_rows = [rows(e) for e in range(4)]
-        last = None
-        for t in range(put.count):
+    def integrate(rows, put, first, end):
+        held_rows = [rows(first + e) for e in range(4)]
+        for t in range(first, end):
             held_rows.append(rows(t + 4))
             total = beams[0] * held_rows[0]
             for j in range(1, 5):
@@ -292,7 +291,7 @@
             put(t, jnp.log(total + 0.05))
             held_rows.pop(0)
 
-    def level_block(half, place):
+    def logs_of(half, place, firsts, ends):
         b, q = block_at(half, place), half * OWN + place
 
         def rows(e):
@@ -303,7 +302,7 @@
             return on[q, 2 * HALO + ROWS - 1 - e].astype(F32)
 
         def put(t, value):
-            logs[t] = value
+            logs[q, t] = value
             row = t - REACH_A
             if 0 <= row < ROWS:
                 rounded = value.astype(BF16)
@@ -312,8 +311,7 @@
                     rounded.astype(F32) * weight_of(row, b)
                 ).astype(BF16)
 
-        put.count = SPAN
-        integrate(rows, put)
+        integrate(rows, put, firsts[0], ends[0])
 
         def edge_rows(e):
             if e < 2:
@@ -327,11 +325,13 @@
         def put_edge(t, value):
             waiting.append(value)
             if t % 2 == 1:
-                logs_edge[t // 2] = jnp.concatenate(waiting, axis=0).astype(BF16)
+                logs_edge[q, t // 2] = jnp.concatenate(waiting, axis=0).astype(BF16)
                 waiting.clear()
 
-        put_edge.count = ROWS
-        integrate(edge_rows, put_edge)
+        integrate(edge_rows, put_edge, firsts[1], ends[1])
+
+    def level_block(half, place):
+        b, q = block_at(half, place), half * OWN + place
 
         means = []
         for group in range(ROWS // GROUP):
@@ -340,7 +340,7 @@
                     center[b, group * GROUP : (group + 1) * GROUP].reshape(
                         GROUP * BINS, LANES
                     ),
-                    logs_edge[group * GROUP // 2 : (group + 1) * GROUP // 2].reshape(
+                    logs_edge[q, group * GROUP // 2 : (group + 1) * GROUP // 2].reshape(
                         GROUP * EDGE, LANES
                     ),
                 ],
@@ -351,21 +351,21 @@
             means.append(jnp.maximum(sums[:size], sums[size:]))
 
         far = REACH_A - 2
-        lead = logs[0]
-        lag = logs[REACH_A + 3]
+        lead = logs[q, 0]
+        lag = logs[q, REACH_A + 3]
         for d in range(1, far):
-            lead = lead + logs[d]
-            lag = lag + logs[REACH_A + 3 + d]
+            lead = lead + logs[q, d]
+            lag = lag + logs[q, REACH_A + 3 + d]
         for row in range(ROWS):
             azimuth = jnp.maximum(
-                lead + near_a * logs[row + far], lag + near_a * logs[row + REACH_A + 2]
+                lead + near_a * logs[q, row + far], lag + near_a * logs[q, row + REACH_A + 2]
             )
             local = row % GROUP
             mean = means[row // GROUP][local * BINS : (local + 1) * BINS]
             level[b, row] = jnp.maximum(azimuth * scale_a, mean * scale_d)
             if row < ROWS - 1:
-                lead = lead + (logs[row + far] - logs[row])
-                lag = lag + (logs[row + REACH_A + 3 + far] - logs[row + REACH_A + 3])
+                lead = lead + (logs[q, row + far] - logs[q, row])
+                lag = lag + (logs[q, row + REACH_A + 3 + far] - logs[q, row + REACH_A + 3])
 
     low = lax.broadcasted_iota(jnp.int32, (8, LANES), 0) < 4
 
@@ -388,11 +388,12 @@
             )
             result[physical(row), :, cells] = ordered.astype(BF16)
 
-    def levels(c, half):
+    def levels(c, half, ends):
         place, size = PIECES[c]
 
         @pl.loop(0, size)
         def _(index):
+            logs_of(half, place + index, (0, 0), ends)
             level_block(half, place + index)
 
     def finishes(c, half):
@@ -420,10 +421,17 @@
             relay(c)
 
     for c in range(len(PIECES)):
+        receive(c, 7, 8)
+
+    @pl.loop(0, OWN)
+    def _(place):
+        logs_of(rd, place, (HALO, 2), (SPAN, ROWS))
+
+    for c in range(len(PIECES)):
         receive(c, 3, 4)
         send(c, 11, 12)
-        receive(c, 9, 10, 7, 8)
-        levels(c, rd)
+        receive(c, 9, 10)
+        levels(c, rd, (HALO, 2))
         if c > 0:
             finishes(c, rd)
 
@@ -432,7 +440,7 @@
             relay(c + AHEAD)
 
         receive(c, 11, 12, 5, 6)
-        levels(c, 1 - rd)
+        levels(c, 1 - rd, (SPAN, ROWS))
         if c == 0:
             finishes(c, rd)
         finishes(c, 1 - rd)
@@ -466,8 +474,8 @@
             pltpu.VMEM((BLOCKS, 2, EDGE, LANES), BF16),
             pltpu.VMEM((BLOCKS, HALO, BINS, LANES), BF16),
             pltpu.VMEM((BLOCKS, 2, EDGE, LANES), BF16),
-            pltpu.VMEM((SPAN, BINS, LANES), F32),
-            pltpu.VMEM((ROWS // 2, BINS, LANES), BF16),
+            pltpu.VMEM((BLOCKS, SPAN, BINS, LANES), F32),
+            pltpu.VMEM((BLOCKS, ROWS // 2, BINS, LANES), BF16),
             pltpu.VMEM((BLOCKS, ROWS, BINS, LANES), BF16),
             pltpu.VMEM((BLOCKS + 2, ROWS, BINS, LANES), BF16),
             pltpu.VMEM((BLOCKS, ROWS, BINS, LANES), F32),

time: 34.3 us -> 33.9 us (0.988)
  Pallas kernels: 33.3 us -> 32.9 us
    pallas_call x1, Pallas kernels: 33.3 us -> 32.9 us  [local(): pl.pallas_call(kernel, out_shape=jax.ShapeDtypeStruct((ROWS, BINS, BLOCKS...]
where the time goes in v6:
time: 33.9 us; the launch traced here: 33.8 us
  Pallas kernels  32.9 us (97%)
  local copies, waits for them, and re-layouts  0.97 us (3%)
    pallas_call x1, Pallas kernels, local(): pl.pallas_call(kernel, out_shape=jax.ShapeDtypeStruct((ROWS, BINS, BLOCKS...  32.9 us
    unnamed x1, local copies, waits for them, and re-layouts  0.97 us

profile of v6, /device:TPU:25, one launch (start us, length us, event | category | flops | bytes accessed | tf_op | source)
XLA Modules:
  0.0 33.8 jit_solution(4297563583951730865)
XLA Ops:
  0.0 32.9 %shard_map.91 = bf16[16,16,2048]{2,1,0:T(8,128)(2,1)S(1)} custom-call(bf16[2,16,32,1024]{3,2,1,0:T(8,128)(2,1)} %echoes.1, f32[1,32]{1,0:T(1,128)} %bitcast.1, f32[64,64]{1,0:T(8,128)} %constant.8.clone.refs_1_, bf16[384,256]{1,0:T(8,128)(2,1)} %constant.9.clone.refs_2_, bf16[256,192]{1,0:T(8,128)(2,1)} %constant.10.clone.refs_3_, ...), custom_call_target="tpu_custom_call" | custom-call | tf_op jit(solution)/shard_map/pallas_call | solution.py:456
  32.9 1.0 %copy.11 = bf16[16,16,2048]{2,1,0:T(8,128)(2,1)} copy(bf16[16,16,2048]{2,1,0:T(8,128)(2,1)S(1)} %shard_map.91) | data formatting | bytes 2097152

commit v7 on v6

--- a/solution.py
+++ b/solution.py
@@ -26,7 +26,7 @@
 SPAN = ROWS + 2 * REACH_A
 ORDER = (0, 1, 2, 3, 12, 13, 14, 15, 4, 5, 6, 7, 8, 9, 10, 11)
 EDGE = 8
-PIECES = ((0, 2), (2, 2), (4, 2), (6, 1), (7, 1))
+PIECES = ((0, 2), (2, 2), (4, 2), (6, 2))
 AHEAD = 2
 PAIR_KINDS, KINDS = 5, 13
 

time: 33.9 us -> 33.5 us (0.988)
  Pallas kernels: 32.9 us -> 32.4 us
    pallas_call x1, Pallas kernels: 32.9 us -> 32.4 us  [local(): pl.pallas_call(kernel, out_shape=jax.ShapeDtypeStruct((ROWS, BINS, BLOCKS...]
where the time goes in v7:
time: 33.5 us; the launch traced here: 33.4 us
  Pallas kernels  32.4 us (97%)
  local copies, waits for them, and re-layouts  0.97 us (3%)
    pallas_call x1, Pallas kernels, local(): pl.pallas_call(kernel, out_shape=jax.ShapeDtypeStruct((ROWS, BINS, BLOCKS...  32.4 us
    unnamed x1, local copies, waits for them, and re-layouts  0.97 us

profile of v7, /device:TPU:25, one launch (start us, length us, event | category | flops | bytes accessed | tf_op | source)
XLA Modules:
  0.0 33.4 jit_solution(13845469734035842404)
XLA Ops:
  0.0 32.4 %shard_map.91 = bf16[16,16,2048]{2,1,0:T(8,128)(2,1)S(1)} custom-call(bf16[2,16,32,1024]{3,2,1,0:T(8,128)(2,1)} %echoes.1, f32[1,32]{1,0:T(1,128)} %bitcast.1, f32[64,64]{1,0:T(8,128)} %constant.8.clone.refs_1_, bf16[384,256]{1,0:T(8,128)(2,1)} %constant.9.clone.refs_2_, bf16[256,192]{1,0:T(8,128)(2,1)} %constant.10.clone.refs_3_, ...), custom_call_target="tpu_custom_call" | custom-call | tf_op jit(solution)/shard_map/pallas_call | solution.py:456
  32.4 1.0 %copy.11 = bf16[16,16,2048]{2,1,0:T(8,128)(2,1)} copy(bf16[16,16,2048]{2,1,0:T(8,128)(2,1)S(1)} %shard_map.91) | data formatting | bytes 2097152
